TPU v7x, 128 devices: a whole 4x4x4 slice. The times are simulated.
128 devices in a mesh: leaf: 4 (over y), rows: 32 (over z, x, core).
Axes of the slice: x: 4, y: 4, z: 4, core: 2. Of those that a mesh axis runs over, the one named last changes fastest.
Arguments:
- leaf_rhs: float32 [8, 16, 2048], P(None, 'leaf', 'rows'), may hold values from -6 to 6
- parent_rhs: float32 [8, 4, 4096], P(None, 'leaf', 'rows'), may hold values from -6 to 6
- root_rhs: float32 [8, 4096], P(None, ('leaf', 'rows')), may hold values from -6 to 6
- leaf_inv: bfloat16 [16, 2048, 2048], P('leaf', 'rows'), as said below
- leaf_panel: bfloat16 [16, 8192, 2048], P('leaf', 'rows'), may hold values from -0.0625 to 0.0625
- leaf_rows: int32 [16, 8192], P('leaf', 'rows'), may hold values from 0 to 8191, as said below
- leaf_height: int32 [16], P('leaf'), may hold values from 2048 to 8192
- parent_inv: bfloat16 [4, 4096, 4096], P('leaf', 'rows'), as said below
- parent_panel: bfloat16 [4, 4096, 4096], P('leaf', 'rows'), may hold values from -0.046875 to 0.046875
- parent_rows: int32 [4, 4096], P('leaf', 'rows'), may hold values from 0 to 4095, as said below
- parent_height: int32 [4], P('leaf'), may hold values from 1024 to 4096
- root_inv: bfloat16 [4096, 4096], P('rows'), as said below
Outputs:
- leaf_solution: float32 [8, 16, 2048], P(None, 'leaf', 'rows')
- parent_solution: float32 [8, 4, 4096], P(None, 'leaf', 'rows')
- root_solution: float32 [8, 4096], P(None, ('leaf', 'rows'))
Inputs may be any that keep to these rules, and one draw needn't show every extreme that they name: `leaf_rows`: each leaf's first leaf_height entries are distinct and ascending; every entry is a valid ancestor index. `parent_rows`: each parent's first parent_height entries are distinct and ascending. `leaf_inv`: A dense well conditioned matrix. `parent_inv`: A dense well conditioned matrix. `root_inv`: A dense well conditioned matrix.
All inputs are finite; a program needn't handle non-finite values.
Results may differ from a plain program's by a relative error of at most 0.009.
Values may be sent and summed in bfloat16 or wider, within the bound.
A program may use at most 64 MiB of HBM per device.

v0:
```python
import jax
import jax.numpy as jnp
from jax import lax
from jax.sharding import PartitionSpec as P


def shards(
    leaf_rhs,
    parent_rhs,
    root_rhs,
    leaf_inv,
    leaf_panel,
    leaf_rows,
    leaf_height,
    parent_inv,
    parent_panel,
    parent_rows,
    parent_height,
    root_inv,
):
    rcount = leaf_rhs.shape[0]
    group_leaves = leaf_rhs.shape[1]
    leaf_local = leaf_panel.shape[1]
    parent_width = parent_inv.shape[2]
    root_width = root_inv.shape[1]
    row_index = lax.axis_index("rows")
    parent_cols = parent_rhs.shape[2]
    root_cols = root_rhs.shape[1]
    flat_index = lax.axis_index("leaf") * lax.axis_size("rows") + row_index
    block = leaf_inv
    ly = jnp.einsum(
        "rln,lin->rli",
        lax.all_gather(leaf_rhs.astype(jnp.bfloat16), "rows", axis=2, tiled=True),
        block,
        preferred_element_type=jnp.float32,
    )
    lyb = ly.astype(jnp.bfloat16)
    block = leaf_panel
    lupd = jnp.einsum(
        "rln,lhn->rlh",
        lax.all_gather(lyb, "rows", axis=2, tiled=True),
        block,
        preferred_element_type=jnp.float32,
    )
    leaf_pos = row_index * leaf_local + jnp.arange(leaf_local, dtype=jnp.int32)
    leaf_mask = leaf_pos[None, :] < leaf_height[:, None]
    lupd = jnp.where(leaf_mask[None, :, :], lupd, 0.0)
    leaf_flat = leaf_rows.reshape(-1)
    local_acc = (
        jnp.zeros((rcount, parent_width + root_width), jnp.float32)
        .at[:, leaf_flat]
        .add(lupd.reshape(rcount, -1))
    )
    group_acc = lax.psum(local_acc, "rows")
    parent_acc = group_acc[:, :parent_width]
    root_from_leaves = lax.psum(group_acc[:, parent_width:], "leaf")
    parent_slice = lax.dynamic_slice_in_dim(parent_acc, row_index * parent_cols, parent_cols, 1)
    prb = (parent_rhs[:, 0, :] - parent_slice).astype(jnp.bfloat16)
    inverse_rows = parent_inv[0]
    panel_rows = parent_panel[0]
    block = inverse_rows
    py = jnp.dot(
        lax.all_gather(prb, "rows", axis=1, tiled=True), block.T, preferred_element_type=jnp.float32
    )
    pyb = py.astype(jnp.bfloat16)
    parent_local = panel_rows.shape[0]
    block = panel_rows
    pupd = jnp.dot(
        lax.all_gather(pyb, "rows", axis=1, tiled=True), block.T, preferred_element_type=jnp.float32
    )
    parent_pos = row_index * parent_local + jnp.arange(parent_local, dtype=jnp.int32)
    parent_mask = parent_pos < parent_height[0]
    pupd = jnp.where(parent_mask[None, :], pupd, 0.0)
    parent_root = jnp.zeros((rcount, root_width), jnp.float32).at[:, parent_rows[0]].add(pupd)
    root_acc = root_from_leaves + lax.psum(parent_root, ("leaf", "rows"))
    root_slice = lax.dynamic_slice_in_dim(root_acc, flat_index * root_cols, root_cols, 1)
    rrb = (root_rhs - root_slice).astype(jnp.bfloat16)
    block = root_inv
    ry = jnp.dot(
        lax.all_gather(rrb, ("leaf", "rows"), axis=1, tiled=True),
        block.T,
        preferred_element_type=jnp.float32,
    )
    root_term = jnp.dot(ry.astype(jnp.bfloat16), root_inv, preferred_element_type=jnp.float32)
    root_full = lax.psum(root_term, "rows")
    root_solution = lax.dynamic_slice_in_dim(root_full, flat_index * root_cols, root_cols, 1)
    rxb = root_full.astype(jnp.bfloat16)
    parent_anc = rxb[:, parent_rows[0]]
    parent_anc = jnp.where(parent_mask[None, :], parent_anc, jnp.zeros_like(parent_anc))
    parent_term = jnp.dot(parent_anc, panel_rows, preferred_element_type=jnp.float32)
    parent_tail = lax.psum_scatter(parent_term, "rows", scatter_dimension=1, tiled=True)
    pvb = (py - parent_tail).astype(jnp.bfloat16)
    parent_sol_term = jnp.dot(pvb, inverse_rows, preferred_element_type=jnp.float32)
    parent_sol = lax.psum_scatter(parent_sol_term, "rows", scatter_dimension=1, tiled=True)
    parent_whole = lax.all_gather(parent_sol.astype(jnp.bfloat16), "rows", axis=1, tiled=True)
    ancestors = jnp.concatenate([parent_whole, rxb], axis=1)
    leaf_anc = ancestors[:, leaf_flat].reshape(rcount, group_leaves, leaf_local)
    leaf_anc = jnp.where(leaf_mask[None, :, :], leaf_anc, jnp.zeros_like(leaf_anc))
    leaf_term = jnp.einsum("rlh,lhc->rlc", leaf_anc, leaf_panel, preferred_element_type=jnp.float32)
    leaf_tail = lax.psum_scatter(leaf_term, "rows", scatter_dimension=2, tiled=True)
    lvb = (ly - leaf_tail).astype(jnp.bfloat16)
    leaf_sol_term = jnp.einsum("rli,lic->rlc", lvb, leaf_inv, preferred_element_type=jnp.float32)
    leaf_sol = lax.psum_scatter(leaf_sol_term, "rows", scatter_dimension=2, tiled=True)
    return (leaf_sol, parent_sol[:, None, :], root_solution)


def solution(mesh):
    return jax.shard_map(
        shards,
        mesh=mesh,
        in_specs=(
            P(None, "leaf", "rows"),
            P(None, "leaf", "rows"),
            P(None, ("leaf", "rows")),
            P("leaf", "rows", None),
            P("leaf", "rows", None),
            P("leaf", "rows"),
            P("leaf"),
            P("leaf", "rows", None),
            P("leaf", "rows", None),
            P("leaf", "rows"),
            P("leaf"),
            P("rows", None),
        ),
        out_specs=(P(None, "leaf", "rows"), P(None, "leaf", "rows"), P(None, ("leaf", "rows"))),
        check_vma=False,
    )
```

profile of v0, /device:TPU:0, one launch (start us, length us, event | category | flops | bytes accessed | tf_op | source)
XLA Modules:
  0.0 916.0 jit_solution(10626270217796478974)
XLA Ops:
  8.9 27.5 %all_gather.18 = bf16[8,4,2048]{0,1,2:T(4,128)(2,1)S(1)} all-gather(bf16[8,4,64]{0,1,2:T(4,128)(2,1)S(1)} %copy.62), channel_id=1, replica_groups=mesh['leaf'=4,'rows'=32] {'rows'}, dimensions={2}, use_global_device_ids=true | all-gather | bytes 135168 | tf_op jit(solution)/shard_map/all_gather | solution.py:33
  37.3 25.3 %all_gather.19 = bf16[8,4,2048]{0,1,2:T(4,128)(2,1)S(1)} all-gather(bf16[8,4,64]{0,1,2:T(4,128)(2,1)S(1)} %copy.64), channel_id=1, replica_groups=mesh['leaf'=4,'rows'=32] {'rows'}, dimensions={2}, use_global_device_ids=true | all-gather | bytes 135168 | tf_op jit(solution)/shard_map/all_gather | solution.py:41
  62.7 3.4 fusion.6
  66.3 8.2 scatter_custom_fusion
  74.5 3.5 copy.67
  78.9 100.7 %all-reduce.5.cloned.1.call-done = f32[8,8192]{1,0:T(8,128)} async-done(((f32[8,8192]{1,0:T(8,128)}), f32[8,8192]{1,0:T(8,128)}) %all-reduce.5.cloned.1.call-update) | async-done | bytes 262160 | tf_op jit(solution)/shard_map/psum | solution.py:54
  181.2 24.6 %all_gather.20 = bf16[8,4096]{1,0:T(8,128)(2,1)S(1)} all-gather(bf16[8,128]{1,0:T(8,128)(2,1)S(1)} %subtract_convert_fusion.3), channel_id=1, replica_groups=mesh['leaf'=4,'rows'=32] {'rows'}, dimensions={1}, use_global_device_ids=true | all-gather | bytes 67584 | tf_op jit(solution)/shard_map/all_gather | solution.py:63
  206.2 21.5 %all_gather.21 = bf16[8,4096]{1,0:T(8,128)(2,1)S(1)} all-gather(bf16[8,128]{1,0:T(8,128)(2,1)S(1)} %get-tuple-element.22), channel_id=1, replica_groups=mesh['leaf'=4,'rows'=32] {'rows'}, dimensions={1}, use_global_device_ids=true | all-gather | bytes 67584 | tf_op jit(solution)/shard_map/all_gather | solution.py:69
  231.8 141.0 %all-reduce.9.cloned.1.call-done = f32[8,4096]{1,0:T(8,128)} async-done(((f32[8,4096]{1,0:T(8,128)}), f32[8,4096]{1,0:T(8,128)}) %all-reduce.9.cloned.1.call-update) | async-done | bytes 131088 | tf_op jit(solution)/shard_map/psum | solution.py:75
  372.8 41.1 %all-reduce.7.cloned.1.call-done = f32[8,4096]{1,0:T(8,128)} async-done(((f32[8,4096]{1,0:T(8,128)}), f32[8,4096]{1,0:T(8,128)}) %all-reduce.7.cloned.1.call-update) | async-done | bytes 131088 | tf_op jit(solution)/shard_map/psum | solution.py:56
  414.7 35.9 %all-gather = bf16[128,32,8]{1,2,0:T(8,128)(2,1)S(1)} all-gather(bf16[1,32,8]{1,2,0:T(8,128)(2,1)S(1)} %fusion.31), channel_id=1, replica_groups=mesh['leaf'=4,'rows'=32] {'leaf','rows'}, dimensions={0}, use_global_device_ids=true | all-gather | bytes 66048 | tf_op jit(solution)/shard_map/all_gather | solution.py:80
  450.9 3.2 fusion.13
  454.2 98.7 %all-reduce.11.cloned.1.call-done = f32[8,4096]{1,0:T(8,128)} async-done(((f32[8,4096]{1,0:T(8,128)}), f32[8,4096]{1,0:T(8,128)}) %all-reduce.11.cloned.1.call-update) | async-done | bytes 131088 | tf_op jit(solution)/shard_map/psum | solution.py:85
  558.2 71.9 %reduce-scatter.9.cloned.1.call-done = f32[8,128]{1,0:T(8,128)} async-done(((f32[8,4096]{1,0:T(8,128)}), f32[8,128]{1,0:T(8,128)}) %reduce-scatter.9.cloned.1.call-update) | async-done | bytes 4112 | tf_op jit(solution)/shard_map/reduce_scatter | solution.py:91
  631.7 73.8 %reduce-scatter.11.cloned.1.call-done = f32[8,128]{1,0:T(8,128)} async-done(((f32[8,4096]{1,0:T(8,128)}), f32[8,128]{1,0:T(8,128)}) %reduce-scatter.11.cloned.1.call-update) | async-done | bytes 4112 | tf_op jit(solution)/shard_map/reduce_scatter | solution.py:94
  706.2 23.5 %all_gather.23 = bf16[8,4096]{1,0:T(8,128)(2,1)S(1)} all-gather(bf16[8,128]{1,0:T(8,128)(2,1)S(1)} %convert_element_type.38), channel_id=1, replica_groups=mesh['leaf'=4,'rows'=32] {'rows'}, dimensions={1}, use_global_device_ids=true | all-gather | bytes 67584 | tf_op jit(solution)/shard_map/all_gather | solution.py:95
  730.7 3.2 gather_fusion.1
  734.1 2.8 convolution_bitcast_fusion.1
  736.9 3.1 copy.76
  740.0 4.5 reshape.143
  744.6 76.7 %reduce-scatter.13.cloned.1.call-done = f32[64,32]{1,0:T(8,128)} async-done(((f32[2048,32]{1,0:T(8,128)}), f32[64,32]{1,0:T(8,128)}) %reduce-scatter.13.cloned.1.call-update) | async-done | bytes 8208
  822.6 3.1 copy.78
  825.6 4.5 reshape.145
  831.6 76.0 %reduce-scatter.15.cloned.1.call-done = f32[64,32]{1,0:T(8,128)} async-done(((f32[2048,32]{1,0:T(8,128)}), f32[64,32]{1,0:T(8,128)}) %reduce-scatter.15.cloned.1.call-update) | async-done | bytes 8208
  (72 shorter events, 23.1 us)
Async XLA Ops:
  7.2 29.2 %copy-start = (bf16[4,64,2048]{2,1,0:T(8,128)(2,1)S(1)}, bf16[4,64,2048]{2,1,0:T(8,128)(2,1)}, u32[]{:S(2)}) copy-start(bf16[4,64,2048]{2,1,0:T(8,128)(2,1)} %param.15) | copy-start | bytes 3145732
  7.2 172.4 %all-reduce.5.cloned.1.call-start = ((), (), s32[]{:S(2)}) async-start(), calls=%async_computation.4 | async-start | bytes 524288 | tf_op jit(solution)/shard_map/psum | solution.py:54
  36.3 26.3 %copy-start.7 = (s32[4]{0:T(128)S(1)}, s32[4]{0:T(128)}, u32[]{:S(2)}) copy-start(s32[4]{0:T(128)} %param.18) | copy-start | bytes 52
  74.5 3.6 copy-start.8
  74.5 106.7 %copy-start.5 = (f32[8,1,128]{2,1,0:T(1,128)S(1)}, f32[8,1,128]{2,1,0:T(1,128)}, u32[]{:S(2)}) copy-start(f32[8,1,128]{2,1,0:T(1,128)} %param.13) | copy-start | bytes 12292
  74.5 131.4 %copy-start.3 = (bf16[1,128,4096]{2,1,0:T(8,128)(2,1)S(1)}, bf16[1,128,4096]{2,1,0:T(8,128)(2,1)}, u32[]{:S(2)}) copy-start(bf16[1,128,4096]{2,1,0:T(8,128)(2,1)} %param.19) | copy-start | bytes 3145732
  78.0 149.7 %copy-start.1 = (bf16[1,128,4096]{2,1,0:T(8,128)(2,1)S(1)}, bf16[1,128,4096]{2,1,0:T(8,128)(2,1)}, u32[]{:S(2)}) copy-start(bf16[1,128,4096]{2,1,0:T(8,128)(2,1)} %param.20) | copy-start | bytes 3145732
  78.1 294.8 %all-reduce.9.cloned.1.call-start = ((), (), s32[]{:S(2)}) async-start(), calls=%async_computation.6 | async-start | bytes 262144 | tf_op jit(solution)/shard_map/psum | solution.py:75
  228.2 185.7 %copy-start.6 = (f32[8,32]{1,0:T(8,128)S(1)}, f32[8,32]{1,0:T(8,128)}, u32[]{:S(2)}) copy-start(f32[8,32]{1,0:T(8,128)} %param.14) | copy-start | bytes 3076
  231.0 182.9 %all-reduce.7.cloned.1.call-start = ((), (), s32[]{:S(2)}) async-start(), calls=%async_computation.5 | async-start | bytes 262144 | tf_op jit(solution)/shard_map/psum | solution.py:56
  231.8 321.1 %all-reduce.11.cloned.1.call-start = ((), (), s32[]{:S(2)}) async-start(), calls=%async_computation.7 | async-start | bytes 262144 | tf_op jit(solution)/shard_map/psum | solution.py:85
  450.6 106.5 %copy-start.2 = (bf16[1,128,4096]{2,1,0:T(8,128)(2,1)S(1)}, bf16[1,128,4096]{2,1,0:T(8,128)(2,1)}, u32[]{:S(2)}) copy-start(bf16[1,128,4096]{2,1,0:T(8,128)(2,1)} %param.20) | copy-start | bytes 3145732
  450.9 179.2 %copy-start.4 = (bf16[1,128,4096]{2,1,0:T(8,128)(2,1)S(1)}, bf16[1,128,4096]{2,1,0:T(8,128)(2,1)}, u32[]{:S(2)}) copy-start(bf16[1,128,4096]{2,1,0:T(8,128)(2,1)} %param.19) | copy-start | bytes 3145732
  454.1 176.0 %reduce-scatter.9.cloned.1.call-start = ((), (), s32[]{:S(2)}) async-start(), calls=%async_computation.8 | async-start | bytes 135168 | tf_op jit(solution)/shard_map/reduce_scatter | solution.py:91
  558.1 147.3 %reduce-scatter.11.cloned.1.call-start = ((), (), s32[]{:S(2)}) async-start(), calls=%async_computation.9 | async-start | bytes 135168 | tf_op jit(solution)/shard_map/reduce_scatter | solution.py:94
  631.7 189.7 %reduce-scatter.13.cloned.1.call-start = ((), (), s32[]{:S(2)}) async-start(), calls=%async_computation.10 | async-start | bytes 1081344
  744.6 163.0 %reduce-scatter.15.cloned.1.call-start = ((), (), s32[]{:S(2)}) async-start(), calls=%async_computation.11 | async-start | bytes 1081344
Sparse Core Ops, SparseCore 0:
  78.2 101.3 all-reduce.4
  231.2 141.6 all-reduce.8
  375.1 38.7 all-reduce.6
  454.2 98.5 all-reduce.10
  558.3 71.7 reduce-scatter.8
  633.9 71.5 reduce-scatter.10
  744.7 76.6 reduce-scatter.12
  830.3 77.2 reduce-scatter.14
where the time goes:
time: 917 us; the launch traced here: 916 us
  waiting for transfers between devices  681 us (74%)
  blocking collectives  158 us (17%)
  local copies, waits for them, and re-layouts  35.6 us (4%)
  between operations  15 us (2%)
  matrix products  13.8 us (2%)
  other arithmetic  12.2 us (1%)
    unnamed x10, waiting for transfers between devices  154 us
    psum x1, waiting for transfers between devices, shards(): root_acc = root_from_leaves + lax.psum(parent_root, ('leaf', 'rows'))  141 us
    psum x1, waiting for transfers between devices, shards(): group_acc = lax.psum(local_acc, 'rows')  101 us
    psum x1, waiting for transfers between devices, shards(): root_full = lax.psum(root_term, 'rows')  98.7 us
    reduce_scatter x1, waiting for transfers between devices, shards(): lax.psum_scatter(parent_sol_term, 'rows', scatter_dimension=1, tiled=True)  73.8 us
    reduce_scatter x1, waiting for transfers between devices, shards(): lax.psum_scatter(parent_term, 'rows', scatter_dimension=1, tiled=True)  71.9 us
    psum x1, waiting for transfers between devices, shards(): root_from_leaves = lax.psum(group_acc[:, parent_width:], 'leaf')  41.1 us
    all_gather x1, blocking collectives, shards(): lax.all_gather(rrb, ('leaf', 'rows'), axis=1, tiled=True)  35.9 us
  transfers between devices with their start and end apart: 8, of which 8 were waited for; matrix products, arithmetic and copies ran while one was open for 0% of the time, Pallas kernels for 0%

commit v1 on v0

--- a/solution.py
+++ b/solution.py
@@ -18,6 +18,19 @@
     parent_height,
     root_inv,
 ):
+
+    def hold_the_units(u_in, axis_key):
+        axis_total = lax.axis_size(axis_key)
+        prior, block_out = (u_in, 0)
+        while 1 << block_out < axis_total:
+            after = range(axis_total)
+            d_next = map(lambda kk: (kk, kk ^ 1 << block_out), after)
+            aux = list(d_next)
+            y = lax.ppermute(prior, axis_name=axis_key, perm=aux)
+            prior = prior + y
+            block_out = block_out + 1
+        return prior
+
     rcount = leaf_rhs.shape[0]
     group_leaves = leaf_rhs.shape[1]
     leaf_local = leaf_panel.shape[1]
@@ -82,7 +95,7 @@
         preferred_element_type=jnp.float32,
     )
     root_term = jnp.dot(ry.astype(jnp.bfloat16), root_inv, preferred_element_type=jnp.float32)
-    root_full = lax.psum(root_term, "rows")
+    root_full = hold_the_units(root_term, "rows")
     root_solution = lax.dynamic_slice_in_dim(root_full, flat_index * root_cols, root_cols, 1)
     rxb = root_full.astype(jnp.bfloat16)
     parent_anc = rxb[:, parent_rows[0]]

time: 917 us -> 841 us (0.917)
  waiting for transfers between devices: 681 us -> 601 us
    psum x1 -> x0, waiting for transfers between devices: 98.7 us -> none  [shards(): root_full = lax.psum(root_term, 'rows')]
    ppermute x0 -> x5, waiting for transfers between devices: none -> 20.4 us  [hold_the_units(): y = lax.ppermute(prior, axis_name=axis_key, perm=aux)]
    unnamed x10 -> x9, waiting for transfers between devices: 154 us -> 154 us
    unnamed x29 -> x31, local copies, waits for them, and re-layouts: 19.6 us -> 19.5 us
  transfers between devices with their start and end apart: 8 -> 12, of which waited for: 8 -> 12; matrix products, arithmetic and copies ran while one was open for 0% -> 0% of each run, Pallas kernels for 0% -> 0%
where the time goes in v1:
time: 841 us; the launch traced here: 840 us
  waiting for transfers between devices  601 us (71%)
  blocking collectives  158 us (19%)
  local copies, waits for them, and re-layouts  35.3 us (4%)
  between operations  15 us (2%)
  matrix products  13.1 us (2%)
  other arithmetic  11.9 us (1%)
    unnamed x9, waiting for transfers between devices  154 us
    psum x1, waiting for transfers between devices, shards(): root_acc = root_from_leaves + lax.psum(parent_root, ('leaf', 'rows'))  141 us
    psum x1, waiting for transfers between devices, shards(): group_acc = lax.psum(local_acc, 'rows')  101 us
    reduce_scatter x1, waiting for transfers between devices, shards(): lax.psum_scatter(parent_sol_term, 'rows', scatter_dimension=1, tiled=True)  73.1 us
    reduce_scatter x1, waiting for transfers between devices, shards(): lax.psum_scatter(parent_term, 'rows', scatter_dimension=1, tiled=True)  70.2 us
    psum x1, waiting for transfers between devices, shards(): root_from_leaves = lax.psum(group_acc[:, parent_width:], 'leaf')  41.1 us
    all_gather x1, blocking collectives, shards(): lax.all_gather(rrb, ('leaf', 'rows'), axis=1, tiled=True)  35.9 us
    all_gather x1, blocking collectives, shards(): lax.all_gather(leaf_rhs.astype(jnp.bfloat16), 'rows', axis=2, tiled=True)  27.5 us
  transfers between devices with their start and end apart: 12, of which 12 were waited for; matrix products, arithmetic and copies ran while one was open for 0% of the time, Pallas kernels for 0%

profile of v1, /device:TPU:0, one launch (start us, length us, event | category | flops | bytes accessed | tf_op | source)
XLA Modules:
  0.0 839.8 jit_solution(9282782583743233189)
XLA Ops:
  8.9 27.5 %all_gather.18 = bf16[8,4,2048]{0,1,2:T(4,128)(2,1)S(1)} all-gather(bf16[8,4,64]{0,1,2:T(4,128)(2,1)S(1)} %copy.62), channel_id=1, replica_groups=mesh['leaf'=4,'rows'=32] {'rows'}, dimensions={2}, use_global_device_ids=true | all-gather | bytes 135168 | tf_op jit(solution)/shard_map/all_gather | solution.py:46
  37.3 25.3 %all_gather.19 = bf16[8,4,2048]{0,1,2:T(4,128)(2,1)S(1)} all-gather(bf16[8,4,64]{0,1,2:T(4,128)(2,1)S(1)} %copy.64), channel_id=1, replica_groups=mesh['leaf'=4,'rows'=32] {'rows'}, dimensions={2}, use_global_device_ids=true | all-gather | bytes 135168 | tf_op jit(solution)/shard_map/all_gather | solution.py:54
  62.7 3.4 fusion.6
  66.3 8.2 scatter_custom_fusion
  74.5 3.5 copy.67
  78.9 100.7 %all-reduce.4.cloned.1.call-done = f32[8,8192]{1,0:T(8,128)} async-done(((f32[8,8192]{1,0:T(8,128)}), f32[8,8192]{1,0:T(8,128)}) %all-reduce.4.cloned.1.call-update) | async-done | bytes 262160 | tf_op jit(solution)/shard_map/psum | solution.py:67
  181.2 24.6 %all_gather.20 = bf16[8,4096]{1,0:T(8,128)(2,1)S(1)} all-gather(bf16[8,128]{1,0:T(8,128)(2,1)S(1)} %subtract_convert_fusion.3), channel_id=1, replica_groups=mesh['leaf'=4,'rows'=32] {'rows'}, dimensions={1}, use_global_device_ids=true | all-gather | bytes 67584 | tf_op jit(solution)/shard_map/all_gather | solution.py:76
  206.2 21.5 %all_gather.21 = bf16[8,4096]{1,0:T(8,128)(2,1)S(1)} all-gather(bf16[8,128]{1,0:T(8,128)(2,1)S(1)} %get-tuple-element.24), channel_id=1, replica_groups=mesh['leaf'=4,'rows'=32] {'rows'}, dimensions={1}, use_global_device_ids=true | all-gather | bytes 67584 | tf_op jit(solution)/shard_map/all_gather | solution.py:82
  231.8 141.0 %all-reduce.8.cloned.1.call-done = f32[8,4096]{1,0:T(8,128)} async-done(((f32[8,4096]{1,0:T(8,128)}), f32[8,4096]{1,0:T(8,128)}) %all-reduce.8.cloned.1.call-update) | async-done | bytes 131088 | tf_op jit(solution)/shard_map/psum | solution.py:88
  372.8 41.1 %all-reduce.6.cloned.1.call-done = f32[8,4096]{1,0:T(8,128)} async-done(((f32[8,4096]{1,0:T(8,128)}), f32[8,4096]{1,0:T(8,128)}) %all-reduce.6.cloned.1.call-update) | async-done | bytes 131088 | tf_op jit(solution)/shard_map/psum | solution.py:69
  414.7 35.9 %all-gather = bf16[128,32,8]{1,2,0:T(8,128)(2,1)S(1)} all-gather(bf16[1,32,8]{1,2,0:T(8,128)(2,1)S(1)} %fusion.31), channel_id=1, replica_groups=mesh['leaf'=4,'rows'=32] {'leaf','rows'}, dimensions={0}, use_global_device_ids=true | all-gather | bytes 66048 | tf_op jit(solution)/shard_map/all_gather | solution.py:93
  455.2 5.4 collective-permute-done.1
  462.5 4.6 collective-permute-done.2
  467.6 4.6 collective-permute-done.3
  474.1 4.7 collective-permute-done.4
  483.3 70.2 %reduce-scatter.9.cloned.1.call-done = f32[8,128]{1,0:T(8,128)} async-done(((f32[8,4096]{1,0:T(8,128)}), f32[8,128]{1,0:T(8,128)}) %reduce-scatter.9.cloned.1.call-update) | async-done | bytes 4112 | tf_op jit(solution)/shard_map/reduce_scatter | solution.py:104
  555.7 73.1 %reduce-scatter.11.cloned.1.call-done = f32[8,128]{1,0:T(8,128)} async-done(((f32[8,4096]{1,0:T(8,128)}), f32[8,128]{1,0:T(8,128)}) %reduce-scatter.11.cloned.1.call-update) | async-done | bytes 4112 | tf_op jit(solution)/shard_map/reduce_scatter | solution.py:107
  629.5 23.6 %all_gather.23 = bf16[8,4096]{1,0:T(8,128)(2,1)S(1)} all-gather(bf16[8,128]{1,0:T(8,128)(2,1)S(1)} %convert_element_type.38), channel_id=1, replica_groups=mesh['leaf'=4,'rows'=32] {'rows'}, dimensions={1}, use_global_device_ids=true | all-gather | bytes 67584 | tf_op jit(solution)/shard_map/all_gather | solution.py:108
  654.1 3.7 gather_fusion.1
  663.8 4.5 reshape.143
  668.5 76.7 %reduce-scatter.13.cloned.1.call-done = f32[64,32]{1,0:T(8,128)} async-done(((f32[2048,32]{1,0:T(8,128)}), f32[64,32]{1,0:T(8,128)}) %reduce-scatter.13.cloned.1.call-update) | async-done | bytes 8208
  746.4 3.1 copy.78
  749.5 4.5 reshape.145
  754.7 76.7 %reduce-scatter.15.cloned.1.call-done = f32[64,32]{1,0:T(8,128)} async-done(((f32[2048,32]{1,0:T(8,128)}), f32[64,32]{1,0:T(8,128)}) %reduce-scatter.15.cloned.1.call-update) | async-done | bytes 8208
  (85 shorter events, 36.5 us)
Async XLA Ops:
  7.2 29.2 %copy-start = (bf16[4,64,2048]{2,1,0:T(8,128)(2,1)S(1)}, bf16[4,64,2048]{2,1,0:T(8,128)(2,1)}, u32[]{:S(2)}) copy-start(bf16[4,64,2048]{2,1,0:T(8,128)(2,1)} %param.15) | copy-start | bytes 3145732
  7.2 172.4 %all-reduce.4.cloned.1.call-start = ((), (), s32[]{:S(2)}) async-start(), calls=%async_computation.4 | async-start | bytes 524288 | tf_op jit(solution)/shard_map/psum | solution.py:67
  36.3 26.3 %copy-start.8 = (s32[4]{0:T(128)S(1)}, s32[4]{0:T(128)}, u32[]{:S(2)}) copy-start(s32[4]{0:T(128)} %param.18) | copy-start | bytes 52
  62.7 3.4 copy-start.5
  74.5 3.6 copy-start.9
  74.5 106.7 %copy-start.6 = (f32[8,1,128]{2,1,0:T(1,128)S(1)}, f32[8,1,128]{2,1,0:T(1,128)}, u32[]{:S(2)}) copy-start(f32[8,1,128]{2,1,0:T(1,128)} %param.13) | copy-start | bytes 12292
  74.5 131.4 %copy-start.3 = (bf16[1,128,4096]{2,1,0:T(8,128)(2,1)S(1)}, bf16[1,128,4096]{2,1,0:T(8,128)(2,1)}, u32[]{:S(2)}) copy-start(bf16[1,128,4096]{2,1,0:T(8,128)(2,1)} %param.19) | copy-start | bytes 3145732
  78.0 149.7 %copy-start.1 = (bf16[1,128,4096]{2,1,0:T(8,128)(2,1)S(1)}, bf16[1,128,4096]{2,1,0:T(8,128)(2,1)}, u32[]{:S(2)}) copy-start(bf16[1,128,4096]{2,1,0:T(8,128)(2,1)} %param.20) | copy-start | bytes 3145732
  78.1 294.7 %all-reduce.8.cloned.1.call-start = ((), (), s32[]{:S(2)}) async-start(), calls=%async_computation.6 | async-start | bytes 262144 | tf_op jit(solution)/shard_map/psum | solution.py:88
  228.2 185.7 %copy-start.7 = (f32[8,32]{1,0:T(8,128)S(1)}, f32[8,32]{1,0:T(8,128)}, u32[]{:S(2)}) copy-start(f32[8,32]{1,0:T(8,128)} %param.14) | copy-start | bytes 3076
  231.0 182.9 %all-reduce.6.cloned.1.call-start = ((), (), s32[]{:S(2)}) async-start(), calls=%async_computation.5 | async-start | bytes 262144 | tf_op jit(solution)/shard_map/psum | solution.py:69
  231.8 321.7 %reduce-scatter.9.cloned.1.call-start = ((), (), s32[]{:S(2)}) async-start(), calls=%async_computation.7 | async-start | bytes 135168 | tf_op jit(solution)/shard_map/reduce_scatter | solution.py:104
  453.3 28.8 %copy-start.2 = (bf16[1,128,4096]{2,1,0:T(8,128)(2,1)S(1)}, bf16[1,128,4096]{2,1,0:T(8,128)(2,1)}, u32[]{:S(2)}) copy-start(bf16[1,128,4096]{2,1,0:T(8,128)(2,1)} %param.20) | copy-start | bytes 3145732
  453.3 1.4 collective-permute-start
  454.7 98.7 %copy-start.4 = (bf16[1,128,4096]{2,1,0:T(8,128)(2,1)S(1)}, bf16[1,128,4096]{2,1,0:T(8,128)(2,1)}, u32[]{:S(2)}) copy-start(bf16[1,128,4096]{2,1,0:T(8,128)(2,1)} %param.19) | copy-start | bytes 3145732
  454.8 5.8 collective-permute-start.1
  460.6 6.6 collective-permute-start.2
  467.2 5.0 collective-permute-start.3
  472.3 6.6 collective-permute-start.4
  483.2 145.6 %reduce-scatter.11.cloned.1.call-start = ((), (), s32[]{:S(2)}) async-start(), calls=%async_computation.8 | async-start | bytes 135168 | tf_op jit(solution)/shard_map/reduce_scatter | solution.py:107
  555.1 190.1 %reduce-scatter.13.cloned.1.call-start = ((), (), s32[]{:S(2)}) async-start(), calls=%async_computation.9 | async-start | bytes 1081344
  668.4 163.0 %reduce-scatter.15.cloned.1.call-start = ((), (), s32[]{:S(2)}) async-start(), calls=%async_computation.10 | async-start | bytes 1081344
Sparse Core Ops, SparseCore 0:
  78.2 101.3 all-reduce.3
  231.2 141.6 all-reduce.7
  375.1 38.7 all-reduce.5
  483.3 70.0 reduce-scatter.8
  557.3 71.4 reduce-scatter.10
  668.5 76.6 reduce-scatter.12
  754.1 77.2 reduce-scatter.14
